TPU v7x, 32 devices: a whole 2x2x4 slice. The times are simulated.
32 devices in a mesh: gx: 8 (over z, core), gy: 4 (over y, x).
Axes of the slice: x: 2, y: 2, z: 4, core: 2. Of those that a mesh axis runs over, the one named last changes fastest.
Arguments:
- init_re: float32 [1, 256, 4096], P(None, 'gx', 'gy'), may hold values from -6 to 6
- init_im: float32 [1, 256, 4096], P(None, 'gx', 'gy'), may hold values from -6 to 6
- onsite: float32 [256, 4096], P('gx', 'gy'), may hold values from -0.9 to 0.9
- bond_x: int32 [256, 4096], P('gx', 'gy'), may hold values from 0 to 15
- bond_y: int32 [256, 4096], P('gx', 'gy'), may hold values from 0 to 15
- hop_table: float32 [16], replicated, may hold values from 1.4 to 1.6
- centre: int32 [1, 2], replicated, may hold values from 0 to 255
- duration: float32 [1], replicated, may hold values from 0.55 to 0.6
Outputs:
- out_re: float32 [1, 256, 4096], P(None, 'gx', 'gy')
- out_im: float32 [1, 256, 4096], P(None, 'gx', 'gy')
- term_norms: float32 [2, 8, 1], replicated
All inputs are finite; a program needn't handle non-finite values.
Results may differ from a plain program's by a relative error of at most 0.0003.
Values sent between devices are 32-bit elements; how exact they have to be, the bound alone decides.
A program may use at most 64 MiB of HBM per device.

v0:
```python
import math
import jax
import jax.numpy as jnp
from jax import lax
from jax.sharding import PartitionSpec as P

TERMS = 8
STEPS = 2
SPECTRAL = 7.5
epsilon = 1e-06


def padded(block, sides, width):
    for axis, dim in sides:
        count = lax.axis_size(axis)
        forward = [(i, i + 1) for i in range(count - 1)]
        forward.append((count - 1, 0))
        backward = [(target, source) for source, target in forward]
        low = lax.ppermute(
            lax.slice_in_dim(block, block.shape[dim] - width, None, axis=dim), axis, forward
        )
        high = lax.ppermute(lax.slice_in_dim(block, 0, width, axis=dim), axis, backward)
        block = jnp.concatenate([low, block, high], axis=dim)
    return block


def bessel_weights(duration):
    argument = duration[0] * SPECTRAL
    halved = argument * 0.5
    weights = []
    for degree in range(TERMS):
        series = halved**degree / math.factorial(degree)
        summed = series
        for counter in range(1, 24):
            series = series * -(halved * halved) / (counter * (counter + degree))
            summed = summed + series
        weights.append(summed if degree == 0 else 2.0 * summed)
    return weights


def rotated(degree, real_part, imag_part):
    quarter = degree % 4
    if quarter == 0:
        return (real_part, imag_part)
    if quarter == 1:
        return (imag_part, -real_part)
    if quarter == 2:
        return (-real_part, -imag_part)
    return (-imag_part, real_part)


def falloff(positions, centres, extent):
    distance = jnp.mod(positions[None, :] - centres[:, None], extent)
    distance = jnp.minimum(distance, extent - distance).astype(jnp.float32)
    return distance * distance * (4.5 / (extent * extent))


def shrink(tensor, margin):
    if margin == 0:
        return tensor
    return tensor[..., margin : tensor.shape[-2] - margin, margin : tensor.shape[-1] - margin]


def apply_wide(grid_field, coeffs):
    potential = coeffs[0]
    hop_rows = coeffs[1]
    hop_cols = coeffs[2]
    result = potential[1:-1, 1:-1] * grid_field[..., 1:-1, 1:-1]
    result = result - hop_rows[1:-1, 1:-1] * grid_field[..., 2:, 1:-1]
    result = result - hop_rows[:-2, 1:-1] * grid_field[..., :-2, 1:-1]
    result = result - hop_cols[1:-1, 1:-1] * grid_field[..., 1:-1, 2:]
    result = result - hop_cols[1:-1, :-2] * grid_field[..., 1:-1, :-2]
    return result * (1.0 / SPECTRAL)


def per_device(init_re, init_im, onsite, bond_x, bond_y, hop_table, centre, duration):
    packets, rows_local, cols_local = init_re.shape
    rows_total = rows_local * lax.axis_size("gx")
    cols_total = cols_local * lax.axis_size("gy")
    cell_count = rows_total * cols_total
    classes = hop_table.shape[0]
    selector = jnp.arange(classes, dtype=jnp.int32)[:, None, None]
    table_column = hop_table[:, None, None]
    hop_down = jnp.sum(jnp.where(bond_x[None] == selector, table_column, 0.0), axis=0)
    hop_right = jnp.sum(jnp.where(bond_y[None] == selector, table_column, 0.0), axis=0)
    weights = bessel_weights(duration)
    row_index = lax.axis_index("gx") * rows_local + lax.iota(jnp.int32, rows_local)
    col_index = lax.axis_index("gy") * cols_local + lax.iota(jnp.int32, cols_local)
    row_fall = falloff(row_index, centre[:, 0], rows_total)
    col_fall = falloff(col_index, centre[:, 1], cols_total)
    envelope = jnp.exp(-(row_fall[:, :, None] + col_fall[:, None, :]))
    packet_state = jnp.stack([init_re * envelope, init_im * envelope])
    reach = TERMS - 1
    coeffs = padded(jnp.stack([onsite, hop_down, hop_right]), (("gx", 1), ("gy", 2)), reach)
    norm_rows = []
    for repeat in range(STEPS):
        current = padded(packet_state, (("gx", 2), ("gy", 3)), reach)
        margin = reach
        previous = current
        previous_margin = reach
        chebyshev = [packet_state]
        for chebyshev_degree in range(1, TERMS):
            applied = apply_wide(current, shrink(coeffs, reach - margin))
            if chebyshev_degree == 1:
                following = applied
            else:
                following = 2.0 * applied - shrink(previous, previous_margin - margin + 1)
            previous, previous_margin = (current, margin)
            current = following
            margin = margin - 1
            chebyshev.append(shrink(following, margin))
        accumulate = weights[0] * packet_state
        for degree in range(1, TERMS):
            real_rot, imag_rot = rotated(degree, chebyshev[degree][0], chebyshev[degree][1])
            accumulate = accumulate + weights[degree] * jnp.stack([real_rot, imag_rot])
        term_local = jnp.stack([jnp.sum(vector * vector, axis=(0, 2, 3)) for vector in chebyshev])
        state_local = jnp.sum(accumulate * accumulate, axis=(0, 2, 3))
        term_total, state_total = lax.psum((term_local, state_local), ("gx", "gy"))
        norm_rows.append(term_total / cell_count)
        rescale = lax.rsqrt(state_total / cell_count + epsilon)
        packet_state = accumulate * rescale[None, :, None, None]
    return (packet_state[0], packet_state[1], jnp.stack(norm_rows))


def solution(mesh):
    return jax.shard_map(
        per_device,
        mesh=mesh,
        in_specs=(
            P(None, "gx", "gy"),
            P(None, "gx", "gy"),
            P("gx", "gy"),
            P("gx", "gy"),
            P("gx", "gy"),
            P(),
            P(),
            P(),
        ),
        out_specs=(P(None, "gx", "gy"), P(None, "gx", "gy"), P()),
        check_vma=False,
    )
```

profile of v0, /device:TPU:0, one launch (start us, length us, event | category | flops | bytes accessed | tf_op | source)
XLA Modules:
  0.0 153.5 jit_solution(4384548073286884623)
XLA Ops:
  0.7 1.3 fusion.128
  2.6 0.7 fusion.97
  3.3 1.1 multiply_bitcast_fusion
  5.0 4.1 %collective-permute-start.5 = (f32[2,1,7,1024]{3,2,1,0:T(8,128)S(1)}, f32[2,1,7,1024]{3,2,1,0:T(8,128)S(1)}, u32[]{:S(2)}, u32[]{:S(2)}) collective-permute-start(f32[2,1,7,1024]{3,2,1,0:T(8,128)S(1)} %get-tuple-element.80), channel_id=1, source_target_pairs={{4,0},{8,4},{12,8},{16,12},{20,16},{24,20},{28,24},{0,28},{5,1},{9... | collective-permute-start | bytes 172040 | tf_op jit(solution)/shard_map/ppermute | solution.py:22
  9.7 3.5 %collective-permute-start.1 = (f32[3,7,1024]{2,1,0:T(8,128)S(1)}, f32[3,7,1024]{2,1,0:T(8,128)S(1)}, u32[]{:S(2)}, u32[]{:S(2)}) collective-permute-start(f32[3,7,1024]{2,1,0:T(8,128)S(1)} %get-tuple-element.52), channel_id=1, source_target_pairs={{4,0},{8,4},{12,8},{16,12},{20,16},{24,20},{28,24},{0,28},{5,1},{9... | collective-permute-start | bytes 258056 | tf_op jit(solution)/shard_map/ppermute | solution.py:22
  14.5 0.7 multiply_reduce_fusion.9
  16.0 3.4 %collective-permute-start.3 = (f32[3,46,7]{2,1,0:T(8,128)S(1)}, f32[3,46,7]{2,1,0:T(8,128)S(1)}, u32[]{:S(2)}, u32[]{:S(2)}) collective-permute-start(f32[3,46,7]{2,1,0:T(8,128)S(1)} %get-tuple-element.39), channel_id=1, source_target_pairs={{1,0},{2,1},{3,2},{0,3},{5,4},{6,5},{7,6},{4,7},{9,8},{10,9},{11,1... | collective-permute-start | bytes 11600 | tf_op jit(solution)/shard_map/ppermute | solution.py:22
  19.4 2.9 %collective-permute-start.7 = (f32[2,1,46,7]{3,2,1,0:T(8,128)S(1)}, f32[2,1,46,7]{3,2,1,0:T(8,128)S(1)}, u32[]{:S(2)}, u32[]{:S(2)}) collective-permute-start(f32[2,1,46,7]{3,2,1,0:T(8,128)S(1)} %get-tuple-element.53), channel_id=1, source_target_pairs={{1,0},{2,1},{3,2},{0,3},{5,4},{6,5},{7,6},{4,7},{9,8},{10,9},{11,1... | collective-permute-start | bytes 7736 | tf_op jit(solution)/shard_map/ppermute | solution.py:22
  22.4 1.8 %collective-permute-done.7 = f32[2,1,46,7]{3,2,1,0:T(8,128)S(1)} collective-permute-done((f32[2,1,46,7]{3,2,1,0:T(8,128)S(1)}, f32[2,1,46,7]{3,2,1,0:T(8,128)S(1)}, u32[]{:S(2)}, u32[]{:S(2)}) %collective-permute-start.7) | collective-permute-done | bytes 2608 | tf_op jit(solution)/shard_map/ppermute | solution.py:22
  24.2 3.2 %collective-permute-done.6 = f32[2,1,46,7]{3,2,1,0:T(8,128)S(1)} collective-permute-done((f32[2,1,46,7]{3,2,1,0:T(8,128)S(1)}, f32[2,1,46,7]{3,2,1,0:T(8,128)S(1)}, u32[]{:S(2)}, u32[]{:S(2)}) %collective-permute-start.6) | collective-permute-done | bytes 2608 | tf_op jit(solution)/shard_map/ppermute | solution.py:19
  30.3 0.8 fusion.65
  32.3 0.8 fusion.64
  38.8 1.1 multiply_reduce_fusion.5
  39.9 0.9 multiply_reduce_fusion.11
  40.8 37.0 %psum.28 = f32[1]{0:T(128)} all-reduce(f32[1]{0:T(128)} %bitcast.29), channel_id=1, replica_groups=mesh['gx'=8,'gy'=4] {'gx','gy'}, use_global_device_ids=true, to_apply=%region_3.4 | all-reduce | flops 1 | bytes 8 | tf_op jit(solution)/shard_map/psum | solution.py:118
  78.5 0.7 multiply_reduce_fusion.4
  79.3 3.5 %collective-permute-start.9 = (f32[2,1,7,1024]{3,2,1,0:T(8,128)S(1)}, f32[2,1,7,1024]{3,2,1,0:T(8,128)S(1)}, u32[]{:S(2)}, u32[]{:S(2)}) collective-permute-start(f32[2,1,7,1024]{3,2,1,0:T(8,128)S(1)} %get-tuple-element.76), channel_id=1, source_target_pairs={{4,0},{8,4},{12,8},{16,12},{20,16},{24,20},{28,24},{0,28},{5,1},{9... | collective-permute-start | bytes 172040 | tf_op jit(solution)/shard_map/ppermute | solution.py:22
  82.8 0.7 fusion.63
  83.5 1.2 collective-permute-done.8
  84.9 2.5 %collective-permute-start.11 = (f32[2,1,46,7]{3,2,1,0:T(8,128)S(1)}, f32[2,1,46,7]{3,2,1,0:T(8,128)S(1)}, u32[]{:S(2)}, u32[]{:S(2)}) collective-permute-start(f32[2,1,46,7]{3,2,1,0:T(8,128)S(1)} %get-tuple-element.49), channel_id=1, source_target_pairs={{1,0},{2,1},{3,2},{0,3},{5,4},{6,5},{7,6},{4,7},{9,8},{10,9},{11,1... | collective-permute-start | bytes 7736 | tf_op jit(solution)/shard_map/ppermute | solution.py:22
  87.4 0.8 multiply_reduce_fusion.8
  88.1 5.1 %stack.171 = f32[8,1]{0,1:T(1,128)S(1)} concatenate(f32[1,1]{0,1:T(1,128)} %bitcast.35, f32[1,1]{0,1:T(1,128)} %bitcast.36, f32[1,1]{0,1:T(1,128)} %bitcast.37, f32[1,1]{0,1:T(1,128)} %bitcast.38, f32[1,1]{0,1:T(1,128)} %bitcast.39, f32[1,1]{0,1:T(1,128)} %bitcast.40, f32[1,1]{0,1:T(1,128)} %bitcast.41, f32[1,1]{0,1:T(1,128)} %bitcast.42), dimensions={0} | concatenate | bytes 64 | tf_op jit(solution)/shard_map/stack | solution.py:116
  93.9 1.1 concatenate.135
  95.5 0.8 fusion.62
  97.0 0.8 fusion.61
  98.4 0.8 fusion.60
  99.8 0.8 multiply_reduce_fusion.3
  103.6 1.0 multiply_reduce_fusion
  105.1 5.2 %stack.181 = f32[8,1]{0,1:T(1,128)S(1)} concatenate(f32[1,1]{0,1:T(1,128)} %bitcast.44, f32[1,1]{0,1:T(1,128)} %bitcast.45, f32[1,1]{0,1:T(1,128)} %bitcast.46, f32[1,1]{0,1:T(1,128)} %bitcast.47, f32[1,1]{0,1:T(1,128)} %bitcast.48, f32[1,1]{0,1:T(1,128)} %bitcast.49, f32[1,1]{0,1:T(1,128)} %bitcast.50, f32[1,1]{0,1:T(1,128)} %bitcast.51), dimensions={0} | concatenate | bytes 64 | tf_op jit(solution)/shard_map/stack | solution.py:116
  110.3 0.8 multiply_reduce_fusion.10
  111.1 40.4 %all-reduce = (f32[1]{0:T(128)}, f32[8,1]{0,1:T(1,128)S(1)}, f32[8,1]{0,1:T(1,128)S(1)}) all-reduce(f32[1]{0:T(128)} %bitcast.31, f32[8,1]{0,1:T(1,128)S(1)} %stack.181, f32[8,1]{0,1:T(1,128)S(1)} %stack.171), channel_id=1, replica_groups=mesh['gx'=8,'gy'=4] {'gx','gy'}, use_global_device_ids=true, to_apply=%region_5.6 | all-reduce | flops 17 | bytes 136 | tf_op jit(solution)/shard_map/psum | solution.py:118
  152.2 0.7 slice_bitcast_fusion.21
  (187 shorter events, 19.0 us)
Async XLA Ops:
  0.6 8.4 %copy-start.54 = (f32[16]{0:T(128)S(1)}, f32[16]{0:T(128)}, u32[]{:S(2)}) copy-start(f32[16]{0:T(128)} %param.13) | copy-start | bytes 196
  0.6 8.4 %copy-start.52 = (s32[32,1024]{1,0:T(8,128)S(1)}, s32[32,1024]{1,0:T(8,128)}, u32[]{:S(2)}) copy-start(s32[32,1024]{1,0:T(8,128)} %param.12) | copy-start | bytes 393220
  0.7 8.4 %copy-start.51 = (s32[32,1024]{1,0:T(8,128)S(1)}, s32[32,1024]{1,0:T(8,128)}, u32[]{:S(2)}) copy-start(s32[32,1024]{1,0:T(8,128)} %param.11) | copy-start | bytes 393220
  3.3 6.3 %copy-start.50 = (f32[32,1024]{1,0:T(8,128)S(1)}, f32[32,1024]{1,0:T(8,128)}, u32[]{:S(2)}) copy-start(f32[32,1024]{1,0:T(8,128)} %param.10) | copy-start | bytes 393220
  4.4 10.8 %collective-permute-start.4 = (f32[2,1,7,1024]{3,2,1,0:T(8,128)S(1)}, f32[2,1,7,1024]{3,2,1,0:T(8,128)S(1)}, u32[]{:S(2)}, u32[]{:S(2)}) collective-permute-start(f32[2,1,7,1024]{3,2,1,0:T(8,128)S(1)} %get-tuple-element.79), channel_id=1, source_target_pairs={{0,4},{4,8},{8,12},{12,16},{16,20},{20,24},{24,28},{28,0},{1,5},{5... | collective-permute-start | bytes 172040 | tf_op jit(solution)/shard_map/ppermute | solution.py:19
  5.0 10.3 %collective-permute-start.5 = (f32[2,1,7,1024]{3,2,1,0:T(8,128)S(1)}, f32[2,1,7,1024]{3,2,1,0:T(8,128)S(1)}, u32[]{:S(2)}, u32[]{:S(2)}) collective-permute-start(f32[2,1,7,1024]{3,2,1,0:T(8,128)S(1)} %get-tuple-element.80), channel_id=1, source_target_pairs={{4,0},{8,4},{12,8},{16,12},{20,16},{24,20},{28,24},{0,28},{5,1},{9... | collective-permute-start | bytes 172040 | tf_op jit(solution)/shard_map/ppermute | solution.py:22
  9.6 6.2 %collective-permute-start = (f32[3,7,1024]{2,1,0:T(8,128)S(1)}, f32[3,7,1024]{2,1,0:T(8,128)S(1)}, u32[]{:S(2)}, u32[]{:S(2)}) collective-permute-start(f32[3,7,1024]{2,1,0:T(8,128)S(1)} %get-tuple-element.51), channel_id=1, source_target_pairs={{0,4},{4,8},{8,12},{12,16},{16,20},{20,24},{24,28},{28,0},{1,5},{5... | collective-permute-start | bytes 258056 | tf_op jit(solution)/shard_map/ppermute | solution.py:19
  9.7 6.1 %collective-permute-start.1 = (f32[3,7,1024]{2,1,0:T(8,128)S(1)}, f32[3,7,1024]{2,1,0:T(8,128)S(1)}, u32[]{:S(2)}, u32[]{:S(2)}) collective-permute-start(f32[3,7,1024]{2,1,0:T(8,128)S(1)} %get-tuple-element.52), channel_id=1, source_target_pairs={{4,0},{8,4},{12,8},{16,12},{20,16},{24,20},{28,24},{0,28},{5,1},{9... | collective-permute-start | bytes 258056 | tf_op jit(solution)/shard_map/ppermute | solution.py:22
  16.0 11.6 %collective-permute-start.3 = (f32[3,46,7]{2,1,0:T(8,128)S(1)}, f32[3,46,7]{2,1,0:T(8,128)S(1)}, u32[]{:S(2)}, u32[]{:S(2)}) collective-permute-start(f32[3,46,7]{2,1,0:T(8,128)S(1)} %get-tuple-element.39), channel_id=1, source_target_pairs={{1,0},{2,1},{3,2},{0,3},{5,4},{6,5},{7,6},{4,7},{9,8},{10,9},{11,1... | collective-permute-start | bytes 11600 | tf_op jit(solution)/shard_map/ppermute | solution.py:22
  19.3 8.2 %collective-permute-start.2 = (f32[3,46,7]{2,1,0:T(8,128)S(1)}, f32[3,46,7]{2,1,0:T(8,128)S(1)}, u32[]{:S(2)}, u32[]{:S(2)}) collective-permute-start(f32[3,46,7]{2,1,0:T(8,128)S(1)} %get-tuple-element.40), channel_id=1, source_target_pairs={{0,1},{1,2},{2,3},{3,0},{4,5},{5,6},{6,7},{7,4},{8,9},{9,10},{10,1... | collective-permute-start | bytes 11600 | tf_op jit(solution)/shard_map/ppermute | solution.py:19
  19.4 4.7 %collective-permute-start.7 = (f32[2,1,46,7]{3,2,1,0:T(8,128)S(1)}, f32[2,1,46,7]{3,2,1,0:T(8,128)S(1)}, u32[]{:S(2)}, u32[]{:S(2)}) collective-permute-start(f32[2,1,46,7]{3,2,1,0:T(8,128)S(1)} %get-tuple-element.53), channel_id=1, source_target_pairs={{1,0},{2,1},{3,2},{0,3},{5,4},{6,5},{7,6},{4,7},{9,8},{10,9},{11,1... | collective-permute-start | bytes 7736 | tf_op jit(solution)/shard_map/ppermute | solution.py:22
  22.4 5.0 %collective-permute-start.6 = (f32[2,1,46,7]{3,2,1,0:T(8,128)S(1)}, f32[2,1,46,7]{3,2,1,0:T(8,128)S(1)}, u32[]{:S(2)}, u32[]{:S(2)}) collective-permute-start(f32[2,1,46,7]{3,2,1,0:T(8,128)S(1)} %get-tuple-element.54), channel_id=1, source_target_pairs={{0,1},{1,2},{2,3},{3,0},{4,5},{5,6},{6,7},{7,4},{8,9},{9,10},{10,1... | collective-permute-start | bytes 7736 | tf_op jit(solution)/shard_map/ppermute | solution.py:19
  33.3 4.3 %copy-start.2 = (f32[34,1026]{1,0:T(8,128)}, f32[34,1026]{1,0:T(8,128)S(1)}, u32[]{:S(2)}) copy-start(f32[34,1026]{1,0:T(8,128)S(1)} %slice.944) | copy-start | bytes 418612
  33.4 2.3 %copy-start.6 = (f32[38,1030]{1,0:T(8,128)}, f32[38,1030]{1,0:T(8,128)S(1)}, u32[]{:S(2)}) copy-start(f32[38,1030]{1,0:T(8,128)S(1)} %slice.914) | copy-start | bytes 469684
  33.6 3.0 %copy-start.4 = (f32[36,1028]{1,0:T(8,128)}, f32[36,1028]{1,0:T(8,128)S(1)}, u32[]{:S(2)}) copy-start(f32[36,1028]{1,0:T(8,128)S(1)} %slice.928) | copy-start | bytes 444100
  79.2 5.5 %collective-permute-start.8 = (f32[2,1,7,1024]{3,2,1,0:T(8,128)S(1)}, f32[2,1,7,1024]{3,2,1,0:T(8,128)S(1)}, u32[]{:S(2)}, u32[]{:S(2)}) collective-permute-start(f32[2,1,7,1024]{3,2,1,0:T(8,128)S(1)} %get-tuple-element.75), channel_id=1, source_target_pairs={{0,4},{4,8},{8,12},{12,16},{16,20},{20,24},{24,28},{28,0},{1,5},{5... | collective-permute-start | bytes 172040 | tf_op jit(solution)/shard_map/ppermute | solution.py:19
  79.3 5.5 %collective-permute-start.9 = (f32[2,1,7,1024]{3,2,1,0:T(8,128)S(1)}, f32[2,1,7,1024]{3,2,1,0:T(8,128)S(1)}, u32[]{:S(2)}, u32[]{:S(2)}) collective-permute-start(f32[2,1,7,1024]{3,2,1,0:T(8,128)S(1)} %get-tuple-element.76), channel_id=1, source_target_pairs={{4,0},{8,4},{12,8},{16,12},{20,16},{24,20},{28,24},{0,28},{5,1},{9... | collective-permute-start | bytes 172040 | tf_op jit(solution)/shard_map/ppermute | solution.py:22
  84.9 8.4 %collective-permute-start.11 = (f32[2,1,46,7]{3,2,1,0:T(8,128)S(1)}, f32[2,1,46,7]{3,2,1,0:T(8,128)S(1)}, u32[]{:S(2)}, u32[]{:S(2)}) collective-permute-start(f32[2,1,46,7]{3,2,1,0:T(8,128)S(1)} %get-tuple-element.49), channel_id=1, source_target_pairs={{1,0},{2,1},{3,2},{0,3},{5,4},{6,5},{7,6},{4,7},{9,8},{10,9},{11,1... | collective-permute-start | bytes 7736 | tf_op jit(solution)/shard_map/ppermute | solution.py:22
  87.4 6.5 %collective-permute-start.10 = (f32[2,1,46,7]{3,2,1,0:T(8,128)S(1)}, f32[2,1,46,7]{3,2,1,0:T(8,128)}, u32[]{:S(2)}, u32[]{:S(2)}) collective-permute-start(f32[2,1,46,7]{3,2,1,0:T(8,128)S(1)} %get-tuple-element.50), channel_id=1, source_target_pairs={{0,1},{1,2},{2,3},{3,0},{4,5},{5,6},{6,7},{7,4},{8,9},{9,10},{10,1... | collective-permute-start | bytes 7736 | tf_op jit(solution)/shard_map/ppermute | solution.py:19
  96.3 1.5 copy-start.9
  96.3 1.5 copy-start.11
  96.3 1.5 copy-start.13
  96.3 1.5 copy-start.15
  96.4 1.5 copy-start.17
  97.8 1.4 copy-start.7
  97.8 1.4 copy-start.35
  97.8 1.4 copy-start.37
  99.2 1.4 copy-start.5
  99.2 1.4 copy-start.19
  99.2 1.4 copy-start.21
  99.3 1.4 copy-start.23
  99.3 1.4 copy-start.25
  (35 other events, 34.8 us)
where the time goes:
time: 154 us
  blocking collectives  77.4 us (50%)
  other arithmetic  23.4 us (15%)
  local copies, waits for them, and re-layouts  21.2 us (14%)
  starting transfers between devices  20.6 us (13%)
  waiting for transfers between devices  6.73 us (4%)
  between operations  4.29 us (3%)
    psum x2, blocking collectives, per_device(): term_total, state_total = lax.psum((term_local, state_local), ('gx', 'gy'))  77.4 us
    ppermute x6, starting transfers between devices, padded(): lax.ppermute(lax.slice_in_dim(block, 0, width, axis=dim), axis, backward)  19.9 us
    another operation x2, local copies, waits for them, and re-layouts, per_device(): jnp.stack([jnp.sum(vector * vector, axis=(0, 2, 3)) for vector in chebysh...  10.4 us
    reduce_sum x12, other arithmetic, per_device(): jnp.sum(vector * vector, axis=(0, 2, 3))  9.75 us
    sub x10, other arithmetic, per_device(): following = 2.0 * applied - shrink(previous, previous_margin - margin + 1)  5.76 us
    ppermute x6, waiting for transfers between devices, padded(): lax.ppermute(lax.slice_in_dim(block, block.shape[dim] - width, None, axis...  4.9 us
    unnamed x110, local copies, waits for them, and re-layouts  3.2 us
  transfers between devices with their start and end apart: 12, of which 4 were waited for; matrix products, arithmetic and copies ran while one was open for 5% of the time, Pallas kernels for 0%

commit v1 on v0

--- a/solution.py
+++ b/solution.py
@@ -8,6 +8,11 @@
 STEPS = 2
 SPECTRAL = 7.5
 epsilon = 1e-06
+
+
+def one_after_other(value, inner_axis, outer_axis):
+    partial = lax.psum(value, inner_axis)
+    return lax.psum(partial, outer_axis)
 
 
 def padded(block, sides, width):
@@ -115,7 +120,7 @@
             accumulate = accumulate + weights[degree] * jnp.stack([real_rot, imag_rot])
         term_local = jnp.stack([jnp.sum(vector * vector, axis=(0, 2, 3)) for vector in chebyshev])
         state_local = jnp.sum(accumulate * accumulate, axis=(0, 2, 3))
-        term_total, state_total = lax.psum((term_local, state_local), ("gx", "gy"))
+        term_total, state_total = one_after_other((term_local, state_local), "gx", "gy")
         norm_rows.append(term_total / cell_count)
         rescale = lax.rsqrt(state_total / cell_count + epsilon)
         packet_state = accumulate * rescale[None, :, None, None]

time: 154 us -> 126 us (0.82)
  blocking collectives: 77.4 us -> 51.3 us
  local copies, waits for them, and re-layouts: 21.2 us -> 19.6 us
    psum x2 -> x4, blocking collectives: 77.4 us -> 51.3 us  [the longest x2 32.2 us: one_after_other(): partial = lax.psum(value, inner_axis)]
    unnamed x110 -> x116, local copies, waits for them, and re-layouts: 3.2 us -> 2.61 us
  transfers between devices with their start and end apart: 12 -> 12, of which waited for: 4 -> 4; matrix products, arithmetic and copies ran while one was open for 5% -> 6% of each run, Pallas kernels for 0% -> 0%
where the time goes in v1:
time: 126 us; the launch traced here: 125 us
  blocking collectives  51.3 us (41%)
  other arithmetic  23.2 us (18%)
  starting transfers between devices  20.1 us (16%)
  local copies, waits for them, and re-layouts  19.6 us (16%)
  waiting for transfers between devices  6.77 us (5%)
  between operations  4.27 us (3%)
    psum x2, blocking collectives, one_after_other(): partial = lax.psum(value, inner_axis)  32.2 us
    psum x2, blocking collectives, one_after_other(): return lax.psum(partial, outer_axis)  19.1 us
    ppermute x6, starting transfers between devices, padded(): lax.ppermute(lax.slice_in_dim(block, 0, width, axis=dim), axis, backward)  19 us
    another operation x2, local copies, waits for them, and re-layouts, per_device(): jnp.stack([jnp.sum(vector * vector, axis=(0, 2, 3)) for vector in chebysh...  10.2 us
    reduce_sum x12, other arithmetic, per_device(): jnp.sum(vector * vector, axis=(0, 2, 3))  9.57 us
    sub x10, other arithmetic, per_device(): following = 2.0 * applied - shrink(previous, previous_margin - margin + 1)  5.79 us
    ppermute x6, waiting for transfers between devices, padded(): lax.ppermute(lax.slice_in_dim(block, block.shape[dim] - width, None, axis...  4.94 us
    unnamed x116, local copies, waits for them, and re-layouts  2.61 us
  transfers between devices with their start and end apart: 12, of which 4 were waited for; matrix products, arithmetic and copies ran while one was open for 6% of the time, Pallas kernels for 0%

profile of v1, /device:TPU:0, one launch (start us, length us, event | category | flops | bytes accessed | tf_op | source)
XLA Modules:
  0.0 125.3 jit_solution(16732381460535738034)
XLA Ops:
  0.7 1.3 %fusion.128 = (s32[1,1]{1,0:T(1,128)}, s32[1,1]{1,0:T(1,128)}) fusion(s32[1,2]{1,0:T(1,128)} %param.14), kind=kLoop, calls=%fused_computation.302 | loop fusion | bytes 16 | tf_op jit(solution)/shard_map/slice | solution.py:94
  3.3 1.1 multiply_bitcast_fusion
  5.0 4.1 %collective-permute-start.5 = (f32[2,1,7,1024]{3,2,1,0:T(8,128)S(1)}, f32[2,1,7,1024]{3,2,1,0:T(8,128)S(1)}, u32[]{:S(2)}, u32[]{:S(2)}) collective-permute-start(f32[2,1,7,1024]{3,2,1,0:T(8,128)S(1)} %get-tuple-element.83), channel_id=1, source_target_pairs={{4,0},{8,4},{12,8},{16,12},{20,16},{24,20},{28,24},{0,28},{5,1},{9... | collective-permute-start | bytes 172040 | tf_op jit(solution)/shard_map/ppermute | solution.py:27
  9.7 3.5 %collective-permute-start.1 = (f32[3,7,1024]{2,1,0:T(8,128)S(1)}, f32[3,7,1024]{2,1,0:T(8,128)S(1)}, u32[]{:S(2)}, u32[]{:S(2)}) collective-permute-start(f32[3,7,1024]{2,1,0:T(8,128)S(1)} %get-tuple-element.55), channel_id=1, source_target_pairs={{4,0},{8,4},{12,8},{16,12},{20,16},{24,20},{28,24},{0,28},{5,1},{9... | collective-permute-start | bytes 258056 | tf_op jit(solution)/shard_map/ppermute | solution.py:27
  16.0 3.4 %collective-permute-start.3 = (f32[3,46,7]{2,1,0:T(8,128)S(1)}, f32[3,46,7]{2,1,0:T(8,128)S(1)}, u32[]{:S(2)}, u32[]{:S(2)}) collective-permute-start(f32[3,46,7]{2,1,0:T(8,128)S(1)} %get-tuple-element.42), channel_id=1, source_target_pairs={{1,0},{2,1},{3,2},{0,3},{5,4},{6,5},{7,6},{4,7},{9,8},{10,9},{11,1... | collective-permute-start | bytes 11600 | tf_op jit(solution)/shard_map/ppermute | solution.py:27
  19.4 2.9 %collective-permute-start.7 = (f32[2,1,46,7]{3,2,1,0:T(8,128)S(1)}, f32[2,1,46,7]{3,2,1,0:T(8,128)S(1)}, u32[]{:S(2)}, u32[]{:S(2)}) collective-permute-start(f32[2,1,46,7]{3,2,1,0:T(8,128)S(1)} %get-tuple-element.56), channel_id=1, source_target_pairs={{1,0},{2,1},{3,2},{0,3},{5,4},{6,5},{7,6},{4,7},{9,8},{10,9},{11,1... | collective-permute-start | bytes 7736 | tf_op jit(solution)/shard_map/ppermute | solution.py:27
  22.4 1.8 %collective-permute-done.7 = f32[2,1,46,7]{3,2,1,0:T(8,128)S(1)} collective-permute-done((f32[2,1,46,7]{3,2,1,0:T(8,128)S(1)}, f32[2,1,46,7]{3,2,1,0:T(8,128)S(1)}, u32[]{:S(2)}, u32[]{:S(2)}) %collective-permute-start.7) | collective-permute-done | bytes 2608 | tf_op jit(solution)/shard_map/ppermute | solution.py:27
  24.2 3.2 %collective-permute-done.6 = f32[2,1,46,7]{3,2,1,0:T(8,128)S(1)} collective-permute-done((f32[2,1,46,7]{3,2,1,0:T(8,128)S(1)}, f32[2,1,46,7]{3,2,1,0:T(8,128)S(1)}, u32[]{:S(2)}, u32[]{:S(2)}) %collective-permute-start.6) | collective-permute-done | bytes 2608 | tf_op jit(solution)/shard_map/ppermute | solution.py:24
  30.3 0.8 fusion.65
  38.0 1.1 multiply_reduce_fusion.5
  39.2 0.9 multiply_reduce_fusion.11
  40.0 15.0 %psum.56 = f32[1]{0:T(128)} all-reduce(f32[1]{0:T(128)} %bitcast.29), channel_id=1, replica_groups=mesh['gx'=8,'gy'=4] {'gx'}, use_global_device_ids=true, to_apply=%region_3.4 | all-reduce | flops 1 | bytes 8 | tf_op jit(solution)/shard_map/psum | solution.py:14
  55.0 0.7 fusion.64
  55.8 8.5 %psum.57 = f32[1]{0:T(128)} all-reduce(f32[1]{0:T(128)} %psum.56), channel_id=1, replica_groups=mesh['gx'=8,'gy'=4] {'gy'}, use_global_device_ids=true, to_apply=%region_4.5 | all-reduce | flops 1 | bytes 8 | tf_op jit(solution)/shard_map/psum | solution.py:15
  65.0 0.7 multiply_reduce_fusion.4
  65.8 3.5 %collective-permute-start.9 = (f32[2,1,7,1024]{3,2,1,0:T(8,128)S(1)}, f32[2,1,7,1024]{3,2,1,0:T(8,128)S(1)}, u32[]{:S(2)}, u32[]{:S(2)}) collective-permute-start(f32[2,1,7,1024]{3,2,1,0:T(8,128)S(1)} %get-tuple-element.79), channel_id=1, source_target_pairs={{4,0},{8,4},{12,8},{16,12},{20,16},{24,20},{28,24},{0,28},{5,1},{9... | collective-permute-start | bytes 172040 | tf_op jit(solution)/shard_map/ppermute | solution.py:27
  69.3 0.8 fusion.63
  70.1 1.2 collective-permute-done.8
  71.4 1.6 %collective-permute-start.11 = (f32[2,1,46,7]{3,2,1,0:T(8,128)S(1)}, f32[2,1,46,7]{3,2,1,0:T(8,128)S(1)}, u32[]{:S(2)}, u32[]{:S(2)}) collective-permute-start(f32[2,1,46,7]{3,2,1,0:T(8,128)S(1)} %get-tuple-element.52), channel_id=1, source_target_pairs={{1,0},{2,1},{3,2},{0,3},{5,4},{6,5},{7,6},{4,7},{9,8},{10,9},{11,1... | collective-permute-start | bytes 7736 | tf_op jit(solution)/shard_map/ppermute | solution.py:27
  73.4 0.7 multiply_reduce_fusion.8
  74.1 5.1 %stack.171 = f32[8,1]{0,1:T(1,128)S(1)} concatenate(f32[1,1]{0,1:T(1,128)} %bitcast.35, f32[1,1]{0,1:T(1,128)} %bitcast.36, f32[1,1]{0,1:T(1,128)} %bitcast.37, f32[1,1]{0,1:T(1,128)} %bitcast.38, f32[1,1]{0,1:T(1,128)} %bitcast.39, f32[1,1]{0,1:T(1,128)} %bitcast.40, f32[1,1]{0,1:T(1,128)} %bitcast.41, f32[1,1]{0,1:T(1,128)} %bitcast.42), dimensions={0} | concatenate | bytes 64 | tf_op jit(solution)/shard_map/stack | solution.py:121
  80.0 0.7 fusion.62
  80.8 0.7 slice_subtract_fusion
  81.5 0.8 fusion.61
  82.9 0.8 fusion.60
  84.3 0.8 multiply_reduce_fusion.3
  88.1 1.0 multiply_reduce_fusion
  89.6 5.2 %stack.181 = f32[8,1]{0,1:T(1,128)S(1)} concatenate(f32[1,1]{0,1:T(1,128)} %bitcast.44, f32[1,1]{0,1:T(1,128)} %bitcast.45, f32[1,1]{0,1:T(1,128)} %bitcast.46, f32[1,1]{0,1:T(1,128)} %bitcast.47, f32[1,1]{0,1:T(1,128)} %bitcast.48, f32[1,1]{0,1:T(1,128)} %bitcast.49, f32[1,1]{0,1:T(1,128)} %bitcast.50, f32[1,1]{0,1:T(1,128)} %bitcast.51), dimensions={0} | concatenate | bytes 64 | tf_op jit(solution)/shard_map/stack | solution.py:121
  94.7 0.8 multiply_reduce_fusion.10
  95.5 17.2 %all-reduce = (f32[1]{0:T(128)}, f32[8,1]{0,1:T(1,128)S(1)}, f32[8,1]{0,1:T(1,128)S(1)}) all-reduce(f32[1]{0:T(128)} %bitcast.31, f32[8,1]{0,1:T(1,128)S(1)} %stack.181, f32[8,1]{0,1:T(1,128)S(1)} %stack.171), channel_id=1, replica_groups=mesh['gx'=8,'gy'=4] {'gx'}, use_global_device_ids=true, to_apply=%region_6.7 | all-reduce | flops 17 | bytes 136 | tf_op jit(solution)/shard_map/psum | solution.py:14
  112.7 10.5 %all-reduce.1 = (f32[1]{0:T(128)}, f32[8,1]{0,1:T(1,128)S(1)}, f32[8,1]{0,1:T(1,128)S(1)}) all-reduce(f32[1]{0:T(128)} %get-tuple-element.5, f32[8,1]{0,1:T(1,128)S(1)} %get-tuple-element.6, f32[8,1]{0,1:T(1,128)S(1)} %get-tuple-element.7), channel_id=1, replica_groups=mesh['gx'=8,'gy'=4] {'gy'}, use_global_device_ids=true, to_apply=%region_7.8 | all-reduce | flops 17 | bytes 136 | tf_op jit(solution)/shard_map/psum | solution.py:15
  124.0 0.7 slice_bitcast_fusion.21
  (195 shorter events, 20.0 us)
Async XLA Ops:
  0.6 8.4 %copy-start.57 = (f32[16]{0:T(128)S(1)}, f32[16]{0:T(128)}, u32[]{:S(2)}) copy-start(f32[16]{0:T(128)} %param.13) | copy-start | bytes 196
  0.6 8.4 %copy-start.56 = (s32[32,1024]{1,0:T(8,128)S(1)}, s32[32,1024]{1,0:T(8,128)}, u32[]{:S(2)}) copy-start(s32[32,1024]{1,0:T(8,128)} %param.12) | copy-start | bytes 393220
  0.7 8.4 %copy-start.55 = (s32[32,1024]{1,0:T(8,128)S(1)}, s32[32,1024]{1,0:T(8,128)}, u32[]{:S(2)}) copy-start(s32[32,1024]{1,0:T(8,128)} %param.11) | copy-start | bytes 393220
  3.3 6.3 %copy-start.54 = (f32[32,1024]{1,0:T(8,128)S(1)}, f32[32,1024]{1,0:T(8,128)}, u32[]{:S(2)}) copy-start(f32[32,1024]{1,0:T(8,128)} %param.10) | copy-start | bytes 393220
  4.4 10.7 %collective-permute-start.4 = (f32[2,1,7,1024]{3,2,1,0:T(8,128)S(1)}, f32[2,1,7,1024]{3,2,1,0:T(8,128)S(1)}, u32[]{:S(2)}, u32[]{:S(2)}) collective-permute-start(f32[2,1,7,1024]{3,2,1,0:T(8,128)S(1)} %get-tuple-element.82), channel_id=1, source_target_pairs={{0,4},{4,8},{8,12},{12,16},{16,20},{20,24},{24,28},{28,0},{1,5},{5... | collective-permute-start | bytes 172040 | tf_op jit(solution)/shard_map/ppermute | solution.py:24
  5.0 10.2 %collective-permute-start.5 = (f32[2,1,7,1024]{3,2,1,0:T(8,128)S(1)}, f32[2,1,7,1024]{3,2,1,0:T(8,128)S(1)}, u32[]{:S(2)}, u32[]{:S(2)}) collective-permute-start(f32[2,1,7,1024]{3,2,1,0:T(8,128)S(1)} %get-tuple-element.83), channel_id=1, source_target_pairs={{4,0},{8,4},{12,8},{16,12},{20,16},{24,20},{28,24},{0,28},{5,1},{9... | collective-permute-start | bytes 172040 | tf_op jit(solution)/shard_map/ppermute | solution.py:27
  9.6 6.2 %collective-permute-start = (f32[3,7,1024]{2,1,0:T(8,128)S(1)}, f32[3,7,1024]{2,1,0:T(8,128)S(1)}, u32[]{:S(2)}, u32[]{:S(2)}) collective-permute-start(f32[3,7,1024]{2,1,0:T(8,128)S(1)} %get-tuple-element.54), channel_id=1, source_target_pairs={{0,4},{4,8},{8,12},{12,16},{16,20},{20,24},{24,28},{28,0},{1,5},{5... | collective-permute-start | bytes 258056 | tf_op jit(solution)/shard_map/ppermute | solution.py:24
  9.7 6.1 %collective-permute-start.1 = (f32[3,7,1024]{2,1,0:T(8,128)S(1)}, f32[3,7,1024]{2,1,0:T(8,128)S(1)}, u32[]{:S(2)}, u32[]{:S(2)}) collective-permute-start(f32[3,7,1024]{2,1,0:T(8,128)S(1)} %get-tuple-element.55), channel_id=1, source_target_pairs={{4,0},{8,4},{12,8},{16,12},{20,16},{24,20},{28,24},{0,28},{5,1},{9... | collective-permute-start | bytes 258056 | tf_op jit(solution)/shard_map/ppermute | solution.py:27
  16.0 11.6 %collective-permute-start.3 = (f32[3,46,7]{2,1,0:T(8,128)S(1)}, f32[3,46,7]{2,1,0:T(8,128)S(1)}, u32[]{:S(2)}, u32[]{:S(2)}) collective-permute-start(f32[3,46,7]{2,1,0:T(8,128)S(1)} %get-tuple-element.42), channel_id=1, source_target_pairs={{1,0},{2,1},{3,2},{0,3},{5,4},{6,5},{7,6},{4,7},{9,8},{10,9},{11,1... | collective-permute-start | bytes 11600 | tf_op jit(solution)/shard_map/ppermute | solution.py:27
  19.3 8.3 %collective-permute-start.2 = (f32[3,46,7]{2,1,0:T(8,128)S(1)}, f32[3,46,7]{2,1,0:T(8,128)S(1)}, u32[]{:S(2)}, u32[]{:S(2)}) collective-permute-start(f32[3,46,7]{2,1,0:T(8,128)S(1)} %get-tuple-element.43), channel_id=1, source_target_pairs={{0,1},{1,2},{2,3},{3,0},{4,5},{5,6},{6,7},{7,4},{8,9},{9,10},{10,1... | collective-permute-start | bytes 11600 | tf_op jit(solution)/shard_map/ppermute | solution.py:24
  19.4 4.7 %collective-permute-start.7 = (f32[2,1,46,7]{3,2,1,0:T(8,128)S(1)}, f32[2,1,46,7]{3,2,1,0:T(8,128)S(1)}, u32[]{:S(2)}, u32[]{:S(2)}) collective-permute-start(f32[2,1,46,7]{3,2,1,0:T(8,128)S(1)} %get-tuple-element.56), channel_id=1, source_target_pairs={{1,0},{2,1},{3,2},{0,3},{5,4},{6,5},{7,6},{4,7},{9,8},{10,9},{11,1... | collective-permute-start | bytes 7736 | tf_op jit(solution)/shard_map/ppermute | solution.py:27
  22.4 5.0 %collective-permute-start.6 = (f32[2,1,46,7]{3,2,1,0:T(8,128)S(1)}, f32[2,1,46,7]{3,2,1,0:T(8,128)S(1)}, u32[]{:S(2)}, u32[]{:S(2)}) collective-permute-start(f32[2,1,46,7]{3,2,1,0:T(8,128)S(1)} %get-tuple-element.57), channel_id=1, source_target_pairs={{0,1},{1,2},{2,3},{3,0},{4,5},{5,6},{6,7},{7,4},{8,9},{9,10},{10,1... | collective-permute-start | bytes 7736 | tf_op jit(solution)/shard_map/ppermute | solution.py:24
  31.4 5.4 %copy-start.6 = (f32[34,1026]{1,0:T(8,128)}, f32[34,1026]{1,0:T(8,128)S(1)}, u32[]{:S(2)}) copy-start(f32[34,1026]{1,0:T(8,128)S(1)} %slice.944) | copy-start | bytes 418612
  31.5 3.4 %copy-start.10 = (f32[38,1030]{1,0:T(8,128)}, f32[38,1030]{1,0:T(8,128)S(1)}, u32[]{:S(2)}) copy-start(f32[38,1030]{1,0:T(8,128)S(1)} %slice.914) | copy-start | bytes 469684
  31.6 4.1 %copy-start.8 = (f32[36,1028]{1,0:T(8,128)}, f32[36,1028]{1,0:T(8,128)S(1)}, u32[]{:S(2)}) copy-start(f32[36,1028]{1,0:T(8,128)S(1)} %slice.928) | copy-start | bytes 444100
  31.8 6.3 %copy-start.44 = (f32[32,1024]{1,0:T(8,128)}, f32[32,1024]{1,0:T(8,128)S(1)}, u32[]{:S(2)}) copy-start(f32[32,1024]{1,0:T(8,128)S(1)} %slice.960) | copy-start | bytes 393220
  31.9 1.6 %copy-start.12 = (f32[40,1032]{1,0:T(8,128)}, f32[40,1032]{1,0:T(8,128)S(1)}, u32[]{:S(2)}) copy-start(f32[40,1032]{1,0:T(8,128)S(1)} %slice.898) | copy-start | bytes 495364
  65.7 5.5 %collective-permute-start.8 = (f32[2,1,7,1024]{3,2,1,0:T(8,128)S(1)}, f32[2,1,7,1024]{3,2,1,0:T(8,128)S(1)}, u32[]{:S(2)}, u32[]{:S(2)}) collective-permute-start(f32[2,1,7,1024]{3,2,1,0:T(8,128)S(1)} %get-tuple-element.78), channel_id=1, source_target_pairs={{0,4},{4,8},{8,12},{12,16},{16,20},{20,24},{24,28},{28,0},{1,5},{5... | collective-permute-start | bytes 172040 | tf_op jit(solution)/shard_map/ppermute | solution.py:24
  65.8 5.5 %collective-permute-start.9 = (f32[2,1,7,1024]{3,2,1,0:T(8,128)S(1)}, f32[2,1,7,1024]{3,2,1,0:T(8,128)S(1)}, u32[]{:S(2)}, u32[]{:S(2)}) collective-permute-start(f32[2,1,7,1024]{3,2,1,0:T(8,128)S(1)} %get-tuple-element.79), channel_id=1, source_target_pairs={{4,0},{8,4},{12,8},{16,12},{20,16},{24,20},{28,24},{0,28},{5,1},{9... | collective-permute-start | bytes 172040 | tf_op jit(solution)/shard_map/ppermute | solution.py:27
  71.4 7.9 %collective-permute-start.11 = (f32[2,1,46,7]{3,2,1,0:T(8,128)S(1)}, f32[2,1,46,7]{3,2,1,0:T(8,128)S(1)}, u32[]{:S(2)}, u32[]{:S(2)}) collective-permute-start(f32[2,1,46,7]{3,2,1,0:T(8,128)S(1)} %get-tuple-element.52), channel_id=1, source_target_pairs={{1,0},{2,1},{3,2},{0,3},{5,4},{6,5},{7,6},{4,7},{9,8},{10,9},{11,1... | collective-permute-start | bytes 7736 | tf_op jit(solution)/shard_map/ppermute | solution.py:27
  72.9 6.3 %collective-permute-start.10 = (f32[2,1,46,7]{3,2,1,0:T(8,128)S(1)}, f32[2,1,46,7]{3,2,1,0:T(8,128)S(1)}, u32[]{:S(2)}, u32[]{:S(2)}) collective-permute-start(f32[2,1,46,7]{3,2,1,0:T(8,128)S(1)} %get-tuple-element.53), channel_id=1, source_target_pairs={{0,1},{1,2},{2,3},{3,0},{4,5},{5,6},{6,7},{7,4},{8,9},{9,10},{10,1... | collective-permute-start | bytes 7736 | tf_op jit(solution)/shard_map/ppermute | solution.py:24
  80.8 1.5 %copy-start.13 = (f32[40,1032]{1,0:T(8,128)S(1)}, f32[40,1032]{1,0:T(8,128)}, u32[]{:S(2)}) copy-start(f32[40,1032]{1,0:T(8,128)} %copy-done.12) | copy-start | bytes 495364
  80.8 1.5 %copy-start.15 = (f32[40,1032]{1,0:T(8,128)S(1)}, f32[40,1032]{1,0:T(8,128)}, u32[]{:S(2)}) copy-start(f32[40,1032]{1,0:T(8,128)} %copy-done.14) | copy-start | bytes 495364
  80.8 1.5 %copy-start.17 = (f32[40,1032]{1,0:T(8,128)S(1)}, f32[40,1032]{1,0:T(8,128)}, u32[]{:S(2)}) copy-start(f32[40,1032]{1,0:T(8,128)} %copy-done.16) | copy-start | bytes 495364
  80.8 1.5 %copy-start.19 = (f32[40,1032]{1,0:T(8,128)S(1)}, f32[40,1032]{1,0:T(8,128)}, u32[]{:S(2)}) copy-start(f32[40,1032]{1,0:T(8,128)} %copy-done.18) | copy-start | bytes 495364
  82.3 1.4 %copy-start.11 = (f32[38,1030]{1,0:T(8,128)S(1)}, f32[38,1030]{1,0:T(8,128)}, u32[]{:S(2)}) copy-start(f32[38,1030]{1,0:T(8,128)} %copy-done.10) | copy-start | bytes 469684
  82.3 1.4 %copy-start.37 = (f32[38,1030]{1,0:T(8,128)S(1)}, f32[38,1030]{1,0:T(8,128)}, u32[]{:S(2)}) copy-start(f32[38,1030]{1,0:T(8,128)} %copy-done.36) | copy-start | bytes 469684
  82.3 1.4 %copy-start.39 = (f32[38,1030]{1,0:T(8,128)S(1)}, f32[38,1030]{1,0:T(8,128)}, u32[]{:S(2)}) copy-start(f32[38,1030]{1,0:T(8,128)} %copy-done.38) | copy-start | bytes 469684
  83.7 1.4 %copy-start.9 = (f32[36,1028]{1,0:T(8,128)S(1)}, f32[36,1028]{1,0:T(8,128)}, u32[]{:S(2)}) copy-start(f32[36,1028]{1,0:T(8,128)} %copy-done.8) | copy-start | bytes 444100
  83.7 1.4 %copy-start.21 = (f32[36,1028]{1,0:T(8,128)S(1)}, f32[36,1028]{1,0:T(8,128)}, u32[]{:S(2)}) copy-start(f32[36,1028]{1,0:T(8,128)} %copy-done.20) | copy-start | bytes 444100
  83.7 1.4 %copy-start.23 = (f32[36,1028]{1,0:T(8,128)S(1)}, f32[36,1028]{1,0:T(8,128)}, u32[]{:S(2)}) copy-start(f32[36,1028]{1,0:T(8,128)} %copy-done.22) | copy-start | bytes 444100
  83.7 1.4 %copy-start.25 = (f32[36,1028]{1,0:T(8,128)S(1)}, f32[36,1028]{1,0:T(8,128)}, u32[]{:S(2)}) copy-start(f32[36,1028]{1,0:T(8,128)} %copy-done.24) | copy-start | bytes 444100
  (38 other events, 38.3 us)
